TPU v7x, 256 devices: a whole 4x4x8 slice. The times are simulated.
256 devices in a mesh: sec: 2 (over x_hi), col: 8 (over y, x_lo), elem: 16 (over z, core).
Axes of the slice: x: 4 (x_hi: 2, x_lo: 2; x = x_hi * 2 + x_lo), y: 4, z: 8, core: 2. Of those that a mesh axis runs over, the one named last changes fastest.
Arguments:
- probes: float32 [256, 96, 256], P('col', 'elem'), may hold values from -6 to 6
- jacobian: float32 [2, 96, 7, 256, 256], P('sec', 'elem'), may hold values from -0.0625 to 0.0625
- neighbors: int32 [96, 7], P('elem'), may hold values from 0 to 95, as said below
- stations: int32 [1024], P('elem'), may hold values from 0 to 95, as said below
- obs_weights: float32 [1024, 256], P('elem'), may hold values from -0.75 to 0.75
Outputs:
- hess_probes: float32 [256, 96, 256], P('col', 'elem', 'sec')
- gram: float32 [256, 256], P('col')
Inputs may be any that keep to these rules, and one draw needn't show every extreme that they name: `neighbors`: row e lists the 7 elements e - 3 to e + 3, taken modulo 96, each once, in an order drawn for each row. Station i lies in one of the 6 elements from (i // 64) * 6 on; every element holds one or more stations.
All inputs are finite; a program needn't handle non-finite values.
Results may differ from a plain program's by a relative error of at most 0.0001.
Values sent between devices are 32-bit elements; how exact they have to be, the bound alone decides.
No kernel may reach another device: no remote copies, remote signals or barrier semaphores. Data moves between devices by JAX's collectives and lax.ppermute only.
A program may use at most 64 MiB of HBM per device.

v0:
```python
import jax
import jax.numpy as jnp
from jax import lax
from jax.sharding import PartitionSpec as P

NBRS = 7
STEPS = 2
PRECISE = lax.Precision.HIGHEST


def with_halo(shard, sides, width):
    for axis, dim in sides:
        devices, length = (lax.axis_size(axis), shard.shape[dim])
        up = [(i, (i + 1) % devices) for i in range(devices)]
        down = [(j, i) for i, j in up]
        last = lax.slice_in_dim(shard, length - width, length, axis=dim)
        leading = lax.slice_in_dim(shard, 0, width, axis=dim)
        before = lax.ppermute(last, axis, up)
        after = lax.ppermute(leading, axis, down)
        shard = jnp.concatenate([before, shard, after], axis=dim)
    return shard


def from_behind(value, axis, steps):
    count = lax.axis_size(axis)
    pairs = [(source, (source + steps) % count) for source in range(count)]
    return lax.ppermute(value, axis, pairs)


def from_behind_2(value, axis, steps):
    count = lax.axis_size(axis)
    leading, last = (max(0, -steps), min(count, count - steps))
    return lax.ppermute(value, axis, [(source, source + steps) for source in range(leading, last)])


def tangent_pass(vector, blocks, lookup, radius):
    column_count, elem_count, dof_count = vector.shape
    for repeat in range(STEPS):
        extended = with_halo(vector, (("elem", 1),), radius)
        gathered = jnp.take(extended, lookup, axis=1).reshape(
            column_count, elem_count, NBRS, dof_count
        )
        vector = vector + jnp.einsum("cekI,ekJI->ceJ", gathered, blocks, precision=PRECISE)
    return vector


def adjoint_pass(vector, blocks, scatter_table, radius):
    column_count, elem_count, dof_count = vector.shape
    for repeat in range(STEPS):
        products = jnp.einsum("ceJ,ekJI->cekI", vector, blocks, precision=PRECISE)
        flattened = products.reshape(column_count, elem_count * NBRS, dof_count)
        extended = jnp.einsum("cxI,xy->cyI", flattened, scatter_table, precision=PRECISE)
        left_rim = extended[:, :radius]
        right_rim = extended[:, elem_count + radius :]
        from_right = from_behind(left_rim, "elem", -1)
        from_left = from_behind(right_rim, "elem", 1)
        centre = extended[:, radius : radius + elem_count]
        centre = centre.at[:, :radius].add(from_left)
        centre = centre.at[:, elem_count - radius :].add(from_right)
        vector = vector + centre
    return vector


def observe(vector, station_table, obs_weights):
    sampled = jnp.einsum("se,ceI->csI", station_table, vector, precision=PRECISE)
    readings = jnp.einsum("csI,sI->cs", sampled, obs_weights, precision=PRECISE)
    weighted = readings[:, :, None] * obs_weights[None, :, :]
    return jnp.einsum("csI,se->ceI", weighted, station_table, precision=PRECISE)


def per_device(probes, jacobian, neighbors, stations, obs_weights):
    column_count, elem_count, dof_count = probes.shape
    radius = (NBRS - 1) // 2
    elem_total = elem_count * lax.axis_size("elem")
    first_elem = lax.axis_index("elem") * elem_count
    lookup = ((neighbors - first_elem + radius) % elem_total).reshape(-1)
    ext_ids = jnp.arange(elem_count + 2 * radius, dtype=jnp.int32)
    scatter_table = (lookup[:, None] == ext_ids[None, :]).astype(jnp.float32)
    local_ids = jnp.arange(elem_count, dtype=jnp.int32)
    station_table = ((stations - first_elem)[:, None] == local_ids[None, :]).astype(jnp.float32)
    segment_index = lax.axis_index("sec")
    leading = segment_index == 0
    half_order = dof_count // 2
    blocks = jacobian[0]
    batch_count = 1
    batch_list = [probes]
    rounds = batch_count + 1
    stored = []
    incoming = jnp.zeros_like(batch_list[0])
    for round_number in range(rounds):
        start_vector = batch_list[min(round_number, batch_count - 1)]
        inputs = jnp.where(leading, start_vector, incoming)
        output = tangent_pass(inputs, blocks, lookup, radius)
        stored.append(output)
        if round_number + 1 < rounds:
            incoming = from_behind_2(output, "sec", 1)
    results = []
    returning = jnp.zeros_like(batch_list[0])
    for round_number in range(rounds):
        state_now = jnp.where(
            leading, stored[max(round_number - 1, 0)], stored[min(round_number + 1, rounds - 1)]
        )
        inputs = returning + observe(state_now, station_table, obs_weights)
        output = adjoint_pass(inputs, blocks, scatter_table, radius)
        if round_number >= 1:
            results.append(output)
        if round_number + 1 < rounds:
            returning = from_behind_2(output, "sec", -1)
    hessian_all = results[0]
    upper_half = from_behind_2(hessian_all[:, :, half_order:], "sec", 1)
    hess_local = jnp.where(leading, hessian_all[:, :, :half_order], upper_half)
    probe_half = lax.dynamic_slice_in_dim(probes, segment_index * half_order, half_order, 2)
    scaling = 1.0 / (elem_total * dof_count)
    shard_piece = lax.all_gather(hess_local, "col", axis=0, tiled=True)
    flat_piece = shard_piece.reshape(shard_piece.shape[0], -1)
    partial_gram = jnp.einsum(
        "ax,bx->ab", probe_half.reshape(column_count, -1), flat_piece, precision=PRECISE
    )
    gram = lax.psum(partial_gram, ("sec", "elem")) * scaling
    return (hess_local, gram)


def solution(mesh):
    in_specs = (
        P("col", "elem", None),
        P("sec", "elem", None, None, None),
        P("elem", None),
        P("elem"),
        P("elem", None),
    )
    out_specs = (P("col", "elem", "sec"), P("col", None))
    return jax.shard_map(
        per_device, mesh=mesh, in_specs=in_specs, out_specs=out_specs, check_vma=False
    )
```

profile of v0, /device:TPU:6, one launch (start us, length us, event | category | flops | bytes accessed | tf_op | source)
XLA Modules:
  0.0 337.1 jit_solution(581083055440860766)
XLA Ops:
  0.7 5.3 %collective-permute-start.1 = (f32[32,3,256]{2,0,1:T(8,128)S(1)}, f32[32,3,256]{2,0,1:T(8,128)S(1)}, u32[]{:S(2)}, u32[]{:S(2)}) collective-permute-start(f32[32,3,256]{2,0,1:T(8,128)S(1)} %get-tuple-element.120), channel_id=1, source_target_pairs={{1,0},{2,1},{3,2},{4,3},{5,4},{6,5},{7,6},{8,7},{9,8},{10,9},{11,1... | collective-permute-start | bytes 294920 | tf_op jit(solution)/shard_map/ppermute | solution.py:19
  6.0 0.7 add_select_fusion
  6.7 0.1 reshape.270
  6.8 1.5 collective-permute-done
  8.3 0.6 gather_fusion
  9.0 0.2 broadcast_select_fusion.3
  9.1 12.6 %fusion.61 = f32[32,6,256]{2,0,1:T(8,128)S(1)} fusion(f32[32,6,256]{2,0,1:T(8,128)S(1)} %broadcast_select_fusion.4, f32[32,6,7,256]{3,0,2,1:T(8,128)S(1)} %bitcast.149, f32[1,6,7,256,256]{4,3,2,1,0:T(8,128)} %param.24), kind=kOutput, calls=%fused_computation.44 | convolution fusion | flops 1057013760 | bytes 12779520 | tf_op jit(solution)/shard_map/cekI,ekJI->ceJ/dot_general | solution.py:43
  21.8 3.0 collective-permute-start.3
  24.8 2.3 collective-permute-done.2
  27.1 0.6 gather_fusion.1
  27.8 0.2 broadcast_select_fusion.2
  28.0 12.7 %fusion.58 = f32[32,6,256]{2,0,1:T(8,128)S(1)} fusion(f32[32,6,256]{2,0,1:T(8,128)S(1)} %fusion.61, f32[32,6,7,256]{3,0,2,1:T(8,128)S(1)} %bitcast.150, f32[1,6,7,256,256]{4,3,2,1,0:T(8,128)} %param.24), kind=kOutput, calls=%fused_computation.43 | convolution fusion | flops 1057013760 | bytes 12779520 | tf_op jit(solution)/shard_map/cekI,ekJI->ceJ/dot_general | solution.py:43
  40.7 1.8 collective-permute-start.4
  42.4 7.3 %collective-permute-done.4 = f32[32,6,256]{2,0,1:T(8,128)S(1)} collective-permute-done((f32[32,6,256]{2,0,1:T(8,128)S(1)}, f32[32,6,256]{2,0,1:T(8,128)S(1)}, u32[]{:S(2)}, u32[]{:S(2)}) %collective-permute-start.4) | collective-permute-done | bytes 196640 | tf_op jit(solution)/shard_map/ppermute | solution.py:33
  49.8 2.9 collective-permute-start.6
  52.7 2.3 collective-permute-done.5
  55.1 0.6 gather_fusion.2
  55.7 0.2 broadcast_select_fusion.1
  55.9 12.6 %fusion.55 = f32[32,6,256]{2,0,1:T(8,128)S(1)} fusion(f32[32,6,256]{2,0,1:T(8,128)S(1)} %broadcast_select_fusion.5, f32[32,6,7,256]{3,0,2,1:T(8,128)S(1)} %bitcast.151, f32[1,6,7,256,256]{4,3,2,1,0:T(8,128)} %param.24), kind=kOutput, calls=%fused_computation.42 | convolution fusion | flops 1057013760 | bytes 12779520 | tf_op jit(solution)/shard_map/cekI,ekJI->ceJ/dot_general | solution.py:43
  68.6 3.0 collective-permute-start.8
  71.6 2.3 collective-permute-done.7
  73.9 0.6 gather_fusion.3
  74.5 0.2 broadcast_select_fusion
  74.7 12.8 %fusion.64 = f32[32,6,256]{2,0,1:T(8,128)S(1)} fusion(f32[32,6,256]{2,0,1:T(8,128)S(1)} %fusion.58, f32[32,6,256]{2,0,1:T(8,128)S(1)} %fusion.55, f32[32,6,7,256]{3,0,2,1:T(8,128)S(1)} %bitcast.148, f32[1,6,7,256,256]{4,3,2,1,0:T(8,128)} %param.24, pred[]{:T(512)S(6)} %eq.16), kind=kOutput, calls=%fused_computation.45 | convolution fusion | flops 1057062912 | bytes 12976129 | tf_op jit(solution)/shard_map/cekI,ekJI->ceJ/dot_general | solution.py:43
  87.5 1.0 convolution_bitcast_fusion
  88.6 3.1 fusion.16
  91.7 0.1 copy.44
  91.7 0.9 fusion.18
  92.7 9.0 %fusion.6 = f32[6,32,7,256]{3,1,2,0:T(8,128)S(1)} fusion(f32[1,6,7,256,256]{4,3,2,1,0:T(8,128)} %param.24, f32[32,6,256,1]{2,1,0,3:T(8,128)S(1)} %bitcast.143), kind=kOutput, calls=%fused_computation.10 | convolution fusion | flops 1056964608 | bytes 12582912 | tf_op jit(solution)/shard_map/ceJ,ekJI->cekI/dot_general | solution.py:50
  101.7 1.4 fusion.28
  103.2 3.0 collective-permute-start.10
  106.2 2.6 collective-permute-done.9
  108.8 0.3 scatter-add.26
  109.1 0.1 slice_add_fusion.6
  109.2 0.3 scatter-add.29
  109.6 9.0 %fusion.4 = f32[6,32,7,256]{3,1,2,0:T(8,128)S(1)} fusion(f32[1,6,7,256,256]{4,3,2,1,0:T(8,128)} %param.24, f32[32,6,256,1]{2,1,0,3:T(8,128)S(1)} %fusion.77), kind=kOutput, calls=%fused_computation.8 | convolution fusion | flops 1056964608 | bytes 12582912 | tf_op jit(solution)/shard_map/ceJ,ekJI->cekI/dot_general | solution.py:50
  118.6 1.4 fusion.31
  120.1 3.0 collective-permute-start.12
  123.0 2.6 collective-permute-done.11
  125.7 0.3 scatter-add.30
  126.0 0.1 slice_add_fusion.4
  126.1 0.3 scatter-add.31
  126.4 1.5 collective-permute-start.13
  127.9 3.9 %collective-permute-done.13 = f32[32,6,256]{2,1,0:T(8,128)S(1)} collective-permute-done((f32[32,6,256]{2,1,0:T(8,128)S(1)}, f32[32,6,256]{2,1,0:T(8,128)S(1)}, u32[]{:S(2)}, u32[]{:S(2)}) %collective-permute-start.13) | collective-permute-done | bytes 196640 | tf_op jit(solution)/shard_map/ppermute | solution.py:33
  131.8 9.2 %fusion.2 = f32[6,32,7,256]{3,1,2,0:T(8,128)S(1)} fusion(f32[1,6,7,256,256]{4,3,2,1,0:T(8,128)} %param.24, f32[32,6,256,1]{2,1,0,3:T(8,128)S(1)} %fusion.75), kind=kOutput, calls=%fused_computation.6 | convolution fusion | flops 1056964608 | bytes 12582912 | tf_op jit(solution)/shard_map/ceJ,ekJI->cekI/dot_general | solution.py:50
  141.0 1.4 fusion.34
  142.5 3.0 collective-permute-start.15
  145.5 2.6 collective-permute-done.14
  148.1 0.3 scatter-add.34
  148.5 0.3 scatter-add.35
  148.9 9.0 %fusion = f32[6,32,7,256]{3,1,2,0:T(8,128)S(1)} fusion(f32[1,6,7,256,256]{4,3,2,1,0:T(8,128)} %param.24, f32[32,6,256,1]{2,1,0,3:T(8,128)S(1)} %fusion.96), kind=kOutput, calls=%fused_computation.4 | convolution fusion | flops 1056964608 | bytes 12582912 | tf_op jit(solution)/shard_map/ceJ,ekJI->cekI/dot_general | solution.py:50
  157.9 1.4 fusion.37
  159.4 3.0 collective-permute-start.17
  162.3 2.6 collective-permute-done.16
  165.0 0.3 scatter-add.36
  165.3 0.1 slice_add_fusion
  165.4 0.3 scatter-add.39
  165.7 0.1 fusion.95
  165.8 1.3 collective-permute-start.18
  167.1 7.6 %collective-permute-done.18 = f32[32,6,128]{2,1,0:T(8,128)S(1)} collective-permute-done((f32[32,6,128]{2,1,0:T(8,128)S(1)}, f32[32,6,128]{2,1,0:T(8,128)S(1)}, u32[]{:S(2)}, u32[]{:S(2)}) %collective-permute-start.18) | collective-permute-done | bytes 98336 | tf_op jit(solution)/shard_map/ppermute | solution.py:33
  174.8 32.1 %all_gather.3 = f32[256,6,128]{2,0,1:T(8,128)S(1)} all-gather(f32[32,6,128]{2,0,1:T(8,128)S(1)} %copy.37), channel_id=1, replica_groups=mesh['sec'=2,'col'=8,'elem'=16] {'col'}, dimensions={0}, use_global_device_ids=true | all-gather | bytes 884736 | tf_op jit(solution)/shard_map/all_gather | solution.py:114
  206.9 0.8 convolution_bitcast_fusion.1
  207.7 128.5 %psum.7 = f32[32,256]{1,0:T(8,128)S(1)} all-reduce(f32[32,256]{1,0:T(8,128)S(1)} %convolution_bitcast_fusion.1), channel_id=1, replica_groups=mesh['sec'=2,'col'=8,'elem'=16] {'sec','elem'}, use_global_device_ids=true, to_apply=%region_0.2 | all-reduce | flops 8192 | bytes 65536 | tf_op jit(solution)/shard_map/psum | solution.py:119
  336.2 0.6 broadcast_multiply_fusion
  (58 shorter events, 1.2 us)
Async XLA Ops:
  0.7 7.6 %collective-permute-start = (f32[32,3,256]{2,0,1:T(8,128)S(1)}, f32[32,3,256]{2,0,1:T(8,128)S(1)}, u32[]{:S(2)}, u32[]{:S(2)}) collective-permute-start(f32[32,3,256]{2,0,1:T(8,128)S(1)} %get-tuple-element.119), channel_id=1, source_target_pairs={{0,1},{1,2},{2,3},{3,4},{4,5},{5,6},{6,7},{7,8},{8,9},{9,10},{10,1... | collective-permute-start | bytes 294920 | tf_op jit(solution)/shard_map/ppermute | solution.py:18
  0.7 7.6 %collective-permute-start.1 = (f32[32,3,256]{2,0,1:T(8,128)S(1)}, f32[32,3,256]{2,0,1:T(8,128)S(1)}, u32[]{:S(2)}, u32[]{:S(2)}) collective-permute-start(f32[32,3,256]{2,0,1:T(8,128)S(1)} %get-tuple-element.120), channel_id=1, source_target_pairs={{1,0},{2,1},{3,2},{4,3},{5,4},{6,5},{7,6},{8,7},{9,8},{10,9},{11,1... | collective-permute-start | bytes 294920 | tf_op jit(solution)/shard_map/ppermute | solution.py:19
  21.8 5.3 %collective-permute-start.2 = (f32[32,3,256]{2,0,1:T(8,128)S(1)}, f32[32,3,256]{2,0,1:T(8,128)S(1)}, u32[]{:S(2)}, u32[]{:S(2)}) collective-permute-start(f32[32,3,256]{2,0,1:T(8,128)S(1)} %get-tuple-element.117), channel_id=1, source_target_pairs={{0,1},{1,2},{2,3},{3,4},{4,5},{5,6},{6,7},{7,8},{8,9},{9,10},{10,1... | collective-permute-start | bytes 294920 | tf_op jit(solution)/shard_map/ppermute | solution.py:18
  21.8 5.3 %collective-permute-start.3 = (f32[32,3,256]{2,0,1:T(8,128)S(1)}, f32[32,3,256]{2,0,1:T(8,128)S(1)}, u32[]{:S(2)}, u32[]{:S(2)}) collective-permute-start(f32[32,3,256]{2,0,1:T(8,128)S(1)} %get-tuple-element.118), channel_id=1, source_target_pairs={{1,0},{2,1},{3,2},{4,3},{5,4},{6,5},{7,6},{8,7},{9,8},{10,9},{11,1... | collective-permute-start | bytes 294920 | tf_op jit(solution)/shard_map/ppermute | solution.py:19
  28.0 21.8 %copy-start = (f32[32,6,256]{2,0,1:T(8,128)S(1)}, f32[32,6,256]{2,0,1:T(8,128)}, u32[]{:S(2)}) copy-start(f32[32,6,256]{2,0,1:T(8,128)} %param.23) | copy-start | bytes 589828
  40.7 9.1 %collective-permute-start.4 = (f32[32,6,256]{2,0,1:T(8,128)S(1)}, f32[32,6,256]{2,0,1:T(8,128)S(1)}, u32[]{:S(2)}, u32[]{:S(2)}) collective-permute-start(f32[32,6,256]{2,0,1:T(8,128)S(1)} %fusion.58), channel_id=1, source_target_pairs={{0,128},{1,129},{2,130},{3,131},{4,132},{5,133},{6,134},{7,135},{8... | collective-permute-start | bytes 589832 | tf_op jit(solution)/shard_map/ppermute | solution.py:33
  49.8 5.3 %collective-permute-start.5 = (f32[32,3,256]{2,0,1:T(8,128)S(1)}, f32[32,3,256]{2,0,1:T(8,128)S(1)}, u32[]{:S(2)}, u32[]{:S(2)}) collective-permute-start(f32[32,3,256]{2,0,1:T(8,128)S(1)} %get-tuple-element.115), channel_id=1, source_target_pairs={{0,1},{1,2},{2,3},{3,4},{4,5},{5,6},{6,7},{7,8},{8,9},{9,10},{10,1... | collective-permute-start | bytes 294920 | tf_op jit(solution)/shard_map/ppermute | solution.py:18
  49.8 5.2 %collective-permute-start.6 = (f32[32,3,256]{2,0,1:T(8,128)S(1)}, f32[32,3,256]{2,0,1:T(8,128)S(1)}, u32[]{:S(2)}, u32[]{:S(2)}) collective-permute-start(f32[32,3,256]{2,0,1:T(8,128)S(1)} %get-tuple-element.116), channel_id=1, source_target_pairs={{1,0},{2,1},{3,2},{4,3},{5,4},{6,5},{7,6},{8,7},{9,8},{10,9},{11,1... | collective-permute-start | bytes 294920 | tf_op jit(solution)/shard_map/ppermute | solution.py:19
  55.9 15.7 %copy-start.3 = (s32[64]{0:T(128)S(1)}, s32[64]{0:T(128)}, u32[]{:S(2)}) copy-start(s32[64]{0:T(128)} %param.26) | copy-start | bytes 772
  68.6 5.3 %collective-permute-start.7 = (f32[32,3,256]{2,0,1:T(8,128)S(1)}, f32[32,3,256]{2,0,1:T(8,128)S(1)}, u32[]{:S(2)}, u32[]{:S(2)}) collective-permute-start(f32[32,3,256]{2,0,1:T(8,128)S(1)} %get-tuple-element.113), channel_id=1, source_target_pairs={{0,1},{1,2},{2,3},{3,4},{4,5},{5,6},{6,7},{7,8},{8,9},{9,10},{10,1... | collective-permute-start | bytes 294920 | tf_op jit(solution)/shard_map/ppermute | solution.py:18
  68.6 5.2 %collective-permute-start.8 = (f32[32,3,256]{2,0,1:T(8,128)S(1)}, f32[32,3,256]{2,0,1:T(8,128)S(1)}, u32[]{:S(2)}, u32[]{:S(2)}) collective-permute-start(f32[32,3,256]{2,0,1:T(8,128)S(1)} %get-tuple-element.114), channel_id=1, source_target_pairs={{1,0},{2,1},{3,2},{4,3},{5,4},{6,5},{7,6},{8,7},{9,8},{10,9},{11,1... | collective-permute-start | bytes 294920 | tf_op jit(solution)/shard_map/ppermute | solution.py:19
  87.5 1.0 copy-start.2
  103.1 5.6 %collective-permute-start.9 = (f32[32,3,256]{2,1,0:T(4,128)S(1)}, f32[32,3,256]{2,1,0:T(4,128)S(1)}, u32[]{:S(2)}, u32[]{:S(2)}) collective-permute-start(f32[32,3,256]{2,1,0:T(4,128)S(1)} %get-tuple-element.112), channel_id=1, source_target_pairs={{0,1},{1,2},{2,3},{3,4},{4,5},{5,6},{6,7},{7,8},{8,9},{9,10},{10,1... | collective-permute-start | bytes 294920 | tf_op jit(solution)/shard_map/ppermute | solution.py:27
  103.2 5.9 %collective-permute-start.10 = (f32[32,3,256]{2,1,0:T(4,128)S(1)}, f32[32,3,256]{2,1,0:T(4,128)S(1)}, u32[]{:S(2)}, u32[]{:S(2)}) collective-permute-start(f32[32,3,256]{2,1,0:T(4,128)S(1)} %get-tuple-element.111), channel_id=1, source_target_pairs={{0,15},{1,0},{2,1},{3,2},{4,3},{5,4},{6,5},{7,6},{8,7},{9,8},{10,9... | collective-permute-start | bytes 294920 | tf_op jit(solution)/shard_map/ppermute | solution.py:27
  120.0 5.6 %collective-permute-start.11 = (f32[32,3,256]{2,1,0:T(4,128)S(1)}, f32[32,3,256]{2,1,0:T(4,128)S(1)}, u32[]{:S(2)}, u32[]{:S(2)}) collective-permute-start(f32[32,3,256]{2,1,0:T(4,128)S(1)} %get-tuple-element.110), channel_id=1, source_target_pairs={{0,1},{1,2},{2,3},{3,4},{4,5},{5,6},{6,7},{7,8},{8,9},{9,10},{10,1... | collective-permute-start | bytes 294920 | tf_op jit(solution)/shard_map/ppermute | solution.py:27
  120.1 5.9 %collective-permute-start.12 = (f32[32,3,256]{2,1,0:T(4,128)S(1)}, f32[32,3,256]{2,1,0:T(4,128)S(1)}, u32[]{:S(2)}, u32[]{:S(2)}) collective-permute-start(f32[32,3,256]{2,1,0:T(4,128)S(1)} %get-tuple-element.109), channel_id=1, source_target_pairs={{0,15},{1,0},{2,1},{3,2},{4,3},{5,4},{6,5},{7,6},{8,7},{9,8},{10,9... | collective-permute-start | bytes 294920 | tf_op jit(solution)/shard_map/ppermute | solution.py:27
  126.4 5.3 %collective-permute-start.13 = (f32[32,6,256]{2,1,0:T(8,128)S(1)}, f32[32,6,256]{2,1,0:T(8,128)S(1)}, u32[]{:S(2)}, u32[]{:S(2)}) collective-permute-start(f32[32,6,256]{2,1,0:T(8,128)S(1)} %fusion.76), channel_id=1, source_target_pairs={{128,0},{129,1},{130,2},{131,3},{132,4},{133,5},{134,6},{135,7},{1... | collective-permute-start | bytes 589832 | tf_op jit(solution)/shard_map/ppermute | solution.py:33
  142.5 5.6 %collective-permute-start.14 = (f32[32,3,256]{2,1,0:T(4,128)S(1)}, f32[32,3,256]{2,1,0:T(4,128)S(1)}, u32[]{:S(2)}, u32[]{:S(2)}) collective-permute-start(f32[32,3,256]{2,1,0:T(4,128)S(1)} %get-tuple-element.108), channel_id=1, source_target_pairs={{0,1},{1,2},{2,3},{3,4},{4,5},{5,6},{6,7},{7,8},{8,9},{9,10},{10,1... | collective-permute-start | bytes 294920 | tf_op jit(solution)/shard_map/ppermute | solution.py:27
  142.5 5.9 %collective-permute-start.15 = (f32[32,3,256]{2,1,0:T(4,128)S(1)}, f32[32,3,256]{2,1,0:T(4,128)S(1)}, u32[]{:S(2)}, u32[]{:S(2)}) collective-permute-start(f32[32,3,256]{2,1,0:T(4,128)S(1)} %get-tuple-element.107), channel_id=1, source_target_pairs={{0,15},{1,0},{2,1},{3,2},{4,3},{5,4},{6,5},{7,6},{8,7},{9,8},{10,9... | collective-permute-start | bytes 294920 | tf_op jit(solution)/shard_map/ppermute | solution.py:27
  159.3 5.6 %collective-permute-start.16 = (f32[32,3,256]{2,1,0:T(4,128)S(1)}, f32[32,3,256]{2,1,0:T(4,128)S(1)}, u32[]{:S(2)}, u32[]{:S(2)}) collective-permute-start(f32[32,3,256]{2,1,0:T(4,128)S(1)} %get-tuple-element.106), channel_id=1, source_target_pairs={{0,1},{1,2},{2,3},{3,4},{4,5},{5,6},{6,7},{7,8},{8,9},{9,10},{10,1... | collective-permute-start | bytes 294920 | tf_op jit(solution)/shard_map/ppermute | solution.py:27
  159.4 5.9 %collective-permute-start.17 = (f32[32,3,256]{2,1,0:T(4,128)S(1)}, f32[32,3,256]{2,1,0:T(4,128)S(1)}, u32[]{:S(2)}, u32[]{:S(2)}) collective-permute-start(f32[32,3,256]{2,1,0:T(4,128)S(1)} %get-tuple-element.105), channel_id=1, source_target_pairs={{0,15},{1,0},{2,1},{3,2},{4,3},{5,4},{6,5},{7,6},{8,7},{9,8},{10,9... | collective-permute-start | bytes 294920 | tf_op jit(solution)/shard_map/ppermute | solution.py:27
  165.8 8.9 %collective-permute-start.18 = (f32[32,6,128]{2,1,0:T(8,128)S(1)}, f32[32,6,128]{2,1,0:T(8,128)S(1)}, u32[]{:S(2)}, u32[]{:S(2)}) collective-permute-start(f32[32,6,128]{2,1,0:T(8,128)S(1)} %slice.329), channel_id=1, source_target_pairs={{0,128},{1,129},{2,130},{3,131},{4,132},{5,133},{6,134},{7,135},{8... | collective-permute-start | bytes 294920 | tf_op jit(solution)/shard_map/ppermute | solution.py:33
  174.8 162.1 %copy-start.1 = (f32[32,6,128]{2,0,1:T(8,128)}, f32[32,6,128]{2,0,1:T(8,128)S(1)}, u32[]{:S(2)}) copy-start(f32[32,6,128]{2,0,1:T(8,128)S(1)} %copy.37) | copy-start | bytes 294916
where the time goes:
time: 344 us; the launch traced here: 337 us
  blocking collectives  161 us (47%)
  matrix products  98.3 us (29%)
  waiting for transfers between devices  37.5 us (11%)
  starting transfers between devices  30.7 us (9%)
  local copies, waits for them, and re-layouts  5.62 us (2%)
    psum x1, blocking collectives, per_device(): gram = lax.psum(partial_gram, ('sec', 'elem')) * scaling  129 us
    dot_general x4, matrix products, tangent_pass(): jnp.einsum('cekI,ekJI->ceJ', gathered, blocks, precision=PRECISE)  50.8 us
    dot_general x4, matrix products, adjoint_pass(): products = jnp.einsum('ceJ,ekJI->cekI', vector, blocks, precision=PRECISE)  36.2 us
    all_gather x1, blocking collectives, per_device(): shard_piece = lax.all_gather(hess_local, 'col', axis=0, tiled=True)  32.1 us
    ppermute x3, waiting for transfers between devices, from_behind_2(): lax.ppermute(value, axis, [(source, source + steps) for source in range(l...  18.8 us
    ppermute x4, starting transfers between devices, with_halo(): after = lax.ppermute(leading, axis, down)  14.2 us
    ppermute x8, starting transfers between devices, from_behind(): return lax.ppermute(value, axis, pairs)  11.9 us
    ppermute x8, waiting for transfers between devices, from_behind(): return lax.ppermute(value, axis, pairs)  10.4 us
  transfers between devices with their start and end apart: 19, of which 11 were waited for; matrix products, arithmetic and copies ran while one was open for 1% of the time, Pallas kernels for 0%

commit v1 on v0

--- a/solution.py
+++ b/solution.py
@@ -111,7 +111,9 @@
     hess_local = jnp.where(leading, hessian_all[:, :, :half_order], upper_half)
     probe_half = lax.dynamic_slice_in_dim(probes, segment_index * half_order, half_order, 2)
     scaling = 1.0 / (elem_total * dof_count)
-    shard_piece = lax.all_gather(hess_local, "col", axis=0, tiled=True)
+    shard_piece = jnp.concatenate(
+        jax.lax.all_to_all(jnp.stack([hess_local] * jax.lax.axis_size("col")), "col", 0, 0), 0
+    )
     flat_piece = shard_piece.reshape(shard_piece.shape[0], -1)
     partial_gram = jnp.einsum(
         "ax,bx->ab", probe_half.reshape(column_count, -1), flat_piece, precision=PRECISE

time: 344 us -> 332 us (0.965)
  the two profiles are of different devices: /device:TPU:6 before, /device:TPU:2 now
where the time goes in v1:
time: 332 us; the launch traced here: 325 us
  blocking collectives  135 us (41%)
  matrix products  98.3 us (30%)
  waiting for transfers between devices  41.3 us (12%)
  starting transfers between devices  38.4 us (12%)
  local copies, waits for them, and re-layouts  7.08 us (2%)
  other arithmetic  3.71 us (1%)
    psum x1, blocking collectives, per_device(): gram = lax.psum(partial_gram, ('sec', 'elem')) * scaling  135 us
    dot_general x4, matrix products, tangent_pass(): jnp.einsum('cekI,ekJI->ceJ', gathered, blocks, precision=PRECISE)  50.8 us
    dot_general x4, matrix products, adjoint_pass(): products = jnp.einsum('ceJ,ekJI->cekI', vector, blocks, precision=PRECISE)  36.2 us
    ppermute x4, starting transfers between devices, with_halo(): after = lax.ppermute(leading, axis, down)  14.2 us
    ppermute x3, waiting for transfers between devices, from_behind_2(): lax.ppermute(value, axis, [(source, source + steps) for source in range(l...  13.7 us
    ppermute x8, starting transfers between devices, from_behind(): return lax.ppermute(value, axis, pairs)  11.9 us
    ppermute x8, waiting for transfers between devices, from_behind(): return lax.ppermute(value, axis, pairs)  10.4 us
    all_to_all x1, waiting for transfers between devices, per_device(): jax.lax.all_to_all(jnp.stack([hess_local] * jax.lax.axis_size('col')), 'c...  8.93 us
  transfers between devices with their start and end apart: 20, of which 12 were waited for; matrix products, arithmetic and copies ran while one was open for 1% of the time, Pallas kernels for 0%

profile of v1, /device:TPU:2, one launch (start us, length us, event | category | flops | bytes accessed | tf_op | source)
XLA Modules:
  0.0 325.4 jit_solution(3133910365934352897)
XLA Ops:
  0.6 0.9 broadcast_select_fusion.4
  1.6 5.3 %collective-permute-start.1 = (f32[32,3,256]{2,0,1:T(8,128)S(1)}, f32[32,3,256]{2,0,1:T(8,128)S(1)}, u32[]{:S(2)}, u32[]{:S(2)}) collective-permute-start(f32[32,3,256]{2,0,1:T(8,128)S(1)} %get-tuple-element.120), channel_id=1, source_target_pairs={{1,0},{2,1},{3,2},{4,3},{5,4},{6,5},{7,6},{8,7},{9,8},{10,9},{11,1... | collective-permute-start | bytes 294920 | tf_op jit(solution)/shard_map/ppermute | solution.py:19
  6.9 0.7 add_select_fusion
  7.6 0.1 reshape.273
  7.8 1.5 collective-permute-done
  9.3 0.6 gather_fusion
  9.9 0.2 broadcast_select_fusion.3
  10.1 12.6 %fusion.61 = f32[32,6,256]{2,0,1:T(8,128)S(1)} fusion(f32[32,6,256]{2,0,1:T(8,128)S(1)} %broadcast_select_fusion.4, f32[32,6,7,256]{3,0,2,1:T(8,128)S(1)} %bitcast.158, f32[1,6,7,256,256]{4,3,2,1,0:T(8,128)} %param.24), kind=kOutput, calls=%fused_computation.44 | convolution fusion | flops 1057013760 | bytes 12779520 | tf_op jit(solution)/shard_map/cekI,ekJI->ceJ/dot_general | solution.py:43
  22.8 3.0 collective-permute-start.3
  25.7 2.3 collective-permute-done.2
  28.1 0.6 gather_fusion.1
  28.7 0.2 broadcast_select_fusion.2
  28.9 12.7 %fusion.58 = f32[32,6,256]{2,0,1:T(8,128)S(1)} fusion(f32[32,6,256]{2,0,1:T(8,128)S(1)} %fusion.61, f32[32,6,7,256]{3,0,2,1:T(8,128)S(1)} %bitcast.159, f32[1,6,7,256,256]{4,3,2,1,0:T(8,128)} %param.24), kind=kOutput, calls=%fused_computation.43 | convolution fusion | flops 1057013760 | bytes 12779520 | tf_op jit(solution)/shard_map/cekI,ekJI->ceJ/dot_general | solution.py:43
  41.6 3.6 %collective-permute-start.4 = (f32[32,6,256]{2,0,1:T(8,128)S(1)}, f32[32,6,256]{2,0,1:T(8,128)S(1)}, u32[]{:S(2)}, u32[]{:S(2)}) collective-permute-start(f32[32,6,256]{2,0,1:T(8,128)S(1)} %fusion.58), channel_id=1, source_target_pairs={{0,128},{1,129},{2,130},{3,131},{4,132},{5,133},{6,134},{7,135},{8... | collective-permute-start | bytes 589832 | tf_op jit(solution)/shard_map/ppermute | solution.py:33
  45.2 2.7 collective-permute-done.4
  47.9 2.9 collective-permute-start.6
  50.9 2.3 collective-permute-done.5
  53.2 0.6 gather_fusion.2
  53.9 0.2 broadcast_select_fusion.1
  54.0 12.6 %fusion.55 = f32[32,6,256]{2,0,1:T(8,128)S(1)} fusion(f32[32,6,256]{2,0,1:T(8,128)S(1)} %broadcast_select_fusion.5, f32[32,6,7,256]{3,0,2,1:T(8,128)S(1)} %bitcast.160, f32[1,6,7,256,256]{4,3,2,1,0:T(8,128)} %param.24), kind=kOutput, calls=%fused_computation.42 | convolution fusion | flops 1057013760 | bytes 12779520 | tf_op jit(solution)/shard_map/cekI,ekJI->ceJ/dot_general | solution.py:43
  66.7 3.0 collective-permute-start.8
  69.7 2.3 collective-permute-done.7
  72.0 0.6 gather_fusion.3
  72.7 0.2 broadcast_select_fusion
  72.8 12.8 %fusion.64 = f32[32,6,256]{2,0,1:T(8,128)S(1)} fusion(f32[32,6,256]{2,0,1:T(8,128)S(1)} %fusion.58, f32[32,6,256]{2,0,1:T(8,128)S(1)} %fusion.55, f32[32,6,7,256]{3,0,2,1:T(8,128)S(1)} %bitcast.157, f32[1,6,7,256,256]{4,3,2,1,0:T(8,128)} %param.24, pred[]{:T(512)S(6)} %eq.16), kind=kOutput, calls=%fused_computation.45 | convolution fusion | flops 1057062912 | bytes 12976129 | tf_op jit(solution)/shard_map/cekI,ekJI->ceJ/dot_general | solution.py:43
  85.7 1.0 convolution_bitcast_fusion
  86.7 3.1 fusion.16
  89.9 0.9 fusion.18
  90.8 9.0 %fusion.6 = f32[6,32,7,256]{3,1,2,0:T(8,128)S(1)} fusion(f32[1,6,7,256,256]{4,3,2,1,0:T(8,128)} %param.24, f32[32,6,256,1]{2,1,0,3:T(8,128)S(1)} %bitcast.152), kind=kOutput, calls=%fused_computation.10 | convolution fusion | flops 1056964608 | bytes 12582912 | tf_op jit(solution)/shard_map/ceJ,ekJI->cekI/dot_general | solution.py:50
  99.8 1.4 fusion.28
  101.3 3.0 collective-permute-start.10
  104.3 2.6 collective-permute-done.9
  106.9 0.3 scatter-add.26
  107.3 0.3 scatter-add.29
  107.7 9.0 %fusion.4 = f32[6,32,7,256]{3,1,2,0:T(8,128)S(1)} fusion(f32[1,6,7,256,256]{4,3,2,1,0:T(8,128)} %param.24, f32[32,6,256,1]{2,1,0,3:T(8,128)S(1)} %fusion.80), kind=kOutput, calls=%fused_computation.8 | convolution fusion | flops 1056964608 | bytes 12582912 | tf_op jit(solution)/shard_map/ceJ,ekJI->cekI/dot_general | solution.py:50
  116.7 1.4 fusion.31
  118.2 3.0 collective-permute-start.12
  121.2 2.6 collective-permute-done.11
  123.8 0.3 scatter-add.30
  124.2 0.3 scatter-add.31
  124.6 1.3 collective-permute-start.13
  125.9 8.5 %collective-permute-done.13 = f32[32,6,256]{2,1,0:T(8,128)S(1)} collective-permute-done((f32[32,6,256]{2,1,0:T(8,128)S(1)}, f32[32,6,256]{2,1,0:T(8,128)S(1)}, u32[]{:S(2)}, u32[]{:S(2)}) %collective-permute-start.13) | collective-permute-done | bytes 196640 | tf_op jit(solution)/shard_map/ppermute | solution.py:33
  134.4 9.2 %fusion.2 = f32[6,32,7,256]{3,1,2,0:T(8,128)S(1)} fusion(f32[1,6,7,256,256]{4,3,2,1,0:T(8,128)} %param.24, f32[32,6,256,1]{2,1,0,3:T(8,128)S(1)} %fusion.78), kind=kOutput, calls=%fused_computation.6 | convolution fusion | flops 1056964608 | bytes 12582912 | tf_op jit(solution)/shard_map/ceJ,ekJI->cekI/dot_general | solution.py:50
  143.6 1.4 fusion.34
  145.1 3.0 collective-permute-start.15
  148.1 2.6 collective-permute-done.14
  150.7 0.3 scatter-add.34
  151.1 0.3 scatter-add.35
  151.5 9.0 %fusion = f32[6,32,7,256]{3,1,2,0:T(8,128)S(1)} fusion(f32[1,6,7,256,256]{4,3,2,1,0:T(8,128)} %param.24, f32[32,6,256,1]{2,1,0,3:T(8,128)S(1)} %fusion.99), kind=kOutput, calls=%fused_computation.4 | convolution fusion | flops 1056964608 | bytes 12582912 | tf_op jit(solution)/shard_map/ceJ,ekJI->cekI/dot_general | solution.py:50
  160.5 1.4 fusion.37
  162.0 3.0 collective-permute-start.17
  164.9 2.6 collective-permute-done.16
  167.6 0.3 scatter-add.36
  168.0 0.3 scatter-add.39
  168.3 0.1 fusion.98
  168.4 1.5 collective-permute-start.18
  169.8 2.5 collective-permute-done.18
  172.4 1.0 stack.2
  173.4 5.9 %all-to-all-start = ((f32[8,32,6,128]{3,1,2,0:T(8,128)}), f32[8,32,6,128]{3,1,2,0:T(8,128)S(1)}, u32[]{:S(2)}, u32[]{:S(2)}) async-start(f32[8,32,6,128]{3,1,2,0:T(8,128)} %stack.2), calls=%async_computation | async-start | bytes 1572864 | tf_op jit(solution)/shard_map/all_to_all | solution.py:115
  179.3 8.9 %all-to-all-done = f32[8,32,6,128]{3,1,2,0:T(8,128)S(1)} async-done(((f32[8,32,6,128]{3,1,2,0:T(8,128)}), f32[8,32,6,128]{3,1,2,0:T(8,128)S(1)}, u32[]{:S(2)}, u32[]{:S(2)}) %all-to-all-start) | async-done | bytes 786464 | tf_op jit(solution)/shard_map/all_to_all | solution.py:115
  188.3 0.5 copy.37
  188.7 0.8 fusion.69
  189.5 135.1 %psum.7 = f32[32,256]{1,0:T(8,128)S(1)} all-reduce(f32[32,256]{1,0:T(8,128)S(1)} %fusion.69), channel_id=1, replica_groups=mesh['sec'=2,'col'=8,'elem'=16] {'sec','elem'}, use_global_device_ids=true, to_apply=%region_0.2 | all-reduce | flops 8192 | bytes 65536 | tf_op jit(solution)/shard_map/psum | solution.py:121
  324.6 0.6 broadcast_multiply_fusion
  (61 shorter events, 1.4 us)
Async XLA Ops:
  1.6 7.6 %collective-permute-start = (f32[32,3,256]{2,0,1:T(8,128)S(1)}, f32[32,3,256]{2,0,1:T(8,128)S(1)}, u32[]{:S(2)}, u32[]{:S(2)}) collective-permute-start(f32[32,3,256]{2,0,1:T(8,128)S(1)} %get-tuple-element.119), channel_id=1, source_target_pairs={{0,1},{1,2},{2,3},{3,4},{4,5},{5,6},{6,7},{7,8},{8,9},{9,10},{10,1... | collective-permute-start | bytes 294920 | tf_op jit(solution)/shard_map/ppermute | solution.py:18
  1.6 7.6 %collective-permute-start.1 = (f32[32,3,256]{2,0,1:T(8,128)S(1)}, f32[32,3,256]{2,0,1:T(8,128)S(1)}, u32[]{:S(2)}, u32[]{:S(2)}) collective-permute-start(f32[32,3,256]{2,0,1:T(8,128)S(1)} %get-tuple-element.120), channel_id=1, source_target_pairs={{1,0},{2,1},{3,2},{4,3},{5,4},{6,5},{7,6},{8,7},{9,8},{10,9},{11,1... | collective-permute-start | bytes 294920 | tf_op jit(solution)/shard_map/ppermute | solution.py:19
  22.7 5.3 %collective-permute-start.2 = (f32[32,3,256]{2,0,1:T(8,128)S(1)}, f32[32,3,256]{2,0,1:T(8,128)S(1)}, u32[]{:S(2)}, u32[]{:S(2)}) collective-permute-start(f32[32,3,256]{2,0,1:T(8,128)S(1)} %get-tuple-element.117), channel_id=1, source_target_pairs={{0,1},{1,2},{2,3},{3,4},{4,5},{5,6},{6,7},{7,8},{8,9},{9,10},{10,1... | collective-permute-start | bytes 294920 | tf_op jit(solution)/shard_map/ppermute | solution.py:18
  22.8 5.3 %collective-permute-start.3 = (f32[32,3,256]{2,0,1:T(8,128)S(1)}, f32[32,3,256]{2,0,1:T(8,128)S(1)}, u32[]{:S(2)}, u32[]{:S(2)}) collective-permute-start(f32[32,3,256]{2,0,1:T(8,128)S(1)} %get-tuple-element.118), channel_id=1, source_target_pairs={{1,0},{2,1},{3,2},{4,3},{5,4},{6,5},{7,6},{8,7},{9,8},{10,9},{11,1... | collective-permute-start | bytes 294920 | tf_op jit(solution)/shard_map/ppermute | solution.py:19
  28.9 19.0 %copy-start = (f32[32,6,256]{2,0,1:T(8,128)S(1)}, f32[32,6,256]{2,0,1:T(8,128)}, u32[]{:S(2)}) copy-start(f32[32,6,256]{2,0,1:T(8,128)} %param.23) | copy-start | bytes 589828
  41.6 6.3 %collective-permute-start.4 = (f32[32,6,256]{2,0,1:T(8,128)S(1)}, f32[32,6,256]{2,0,1:T(8,128)S(1)}, u32[]{:S(2)}, u32[]{:S(2)}) collective-permute-start(f32[32,6,256]{2,0,1:T(8,128)S(1)} %fusion.58), channel_id=1, source_target_pairs={{0,128},{1,129},{2,130},{3,131},{4,132},{5,133},{6,134},{7,135},{8... | collective-permute-start | bytes 589832 | tf_op jit(solution)/shard_map/ppermute | solution.py:33
  47.9 5.3 %collective-permute-start.5 = (f32[32,3,256]{2,0,1:T(8,128)S(1)}, f32[32,3,256]{2,0,1:T(8,128)S(1)}, u32[]{:S(2)}, u32[]{:S(2)}) collective-permute-start(f32[32,3,256]{2,0,1:T(8,128)S(1)} %get-tuple-element.115), channel_id=1, source_target_pairs={{0,1},{1,2},{2,3},{3,4},{4,5},{5,6},{6,7},{7,8},{8,9},{9,10},{10,1... | collective-permute-start | bytes 294920 | tf_op jit(solution)/shard_map/ppermute | solution.py:18
  47.9 5.2 %collective-permute-start.6 = (f32[32,3,256]{2,0,1:T(8,128)S(1)}, f32[32,3,256]{2,0,1:T(8,128)S(1)}, u32[]{:S(2)}, u32[]{:S(2)}) collective-permute-start(f32[32,3,256]{2,0,1:T(8,128)S(1)} %get-tuple-element.116), channel_id=1, source_target_pairs={{1,0},{2,1},{3,2},{4,3},{5,4},{6,5},{7,6},{8,7},{9,8},{10,9},{11,1... | collective-permute-start | bytes 294920 | tf_op jit(solution)/shard_map/ppermute | solution.py:19
  54.0 15.7 %copy-start.3 = (s32[64]{0:T(128)S(1)}, s32[64]{0:T(128)}, u32[]{:S(2)}) copy-start(s32[64]{0:T(128)} %param.26) | copy-start | bytes 772
  66.7 5.3 %collective-permute-start.7 = (f32[32,3,256]{2,0,1:T(8,128)S(1)}, f32[32,3,256]{2,0,1:T(8,128)S(1)}, u32[]{:S(2)}, u32[]{:S(2)}) collective-permute-start(f32[32,3,256]{2,0,1:T(8,128)S(1)} %get-tuple-element.113), channel_id=1, source_target_pairs={{0,1},{1,2},{2,3},{3,4},{4,5},{5,6},{6,7},{7,8},{8,9},{9,10},{10,1... | collective-permute-start | bytes 294920 | tf_op jit(solution)/shard_map/ppermute | solution.py:18
  66.7 5.2 %collective-permute-start.8 = (f32[32,3,256]{2,0,1:T(8,128)S(1)}, f32[32,3,256]{2,0,1:T(8,128)S(1)}, u32[]{:S(2)}, u32[]{:S(2)}) collective-permute-start(f32[32,3,256]{2,0,1:T(8,128)S(1)} %get-tuple-element.114), channel_id=1, source_target_pairs={{1,0},{2,1},{3,2},{4,3},{5,4},{6,5},{7,6},{8,7},{9,8},{10,9},{11,1... | collective-permute-start | bytes 294920 | tf_op jit(solution)/shard_map/ppermute | solution.py:19
  85.7 1.1 copy-start.2
  101.3 5.6 %collective-permute-start.9 = (f32[32,3,256]{2,1,0:T(4,128)S(1)}, f32[32,3,256]{2,1,0:T(4,128)S(1)}, u32[]{:S(2)}, u32[]{:S(2)}) collective-permute-start(f32[32,3,256]{2,1,0:T(4,128)S(1)} %get-tuple-element.112), channel_id=1, source_target_pairs={{0,1},{1,2},{2,3},{3,4},{4,5},{5,6},{6,7},{7,8},{8,9},{9,10},{10,1... | collective-permute-start | bytes 294920 | tf_op jit(solution)/shard_map/ppermute | solution.py:27
  101.3 5.9 %collective-permute-start.10 = (f32[32,3,256]{2,1,0:T(4,128)S(1)}, f32[32,3,256]{2,1,0:T(4,128)S(1)}, u32[]{:S(2)}, u32[]{:S(2)}) collective-permute-start(f32[32,3,256]{2,1,0:T(4,128)S(1)} %get-tuple-element.111), channel_id=1, source_target_pairs={{0,15},{1,0},{2,1},{3,2},{4,3},{5,4},{6,5},{7,6},{8,7},{9,8},{10,9... | collective-permute-start | bytes 294920 | tf_op jit(solution)/shard_map/ppermute | solution.py:27
  118.1 5.6 %collective-permute-start.11 = (f32[32,3,256]{2,1,0:T(4,128)S(1)}, f32[32,3,256]{2,1,0:T(4,128)S(1)}, u32[]{:S(2)}, u32[]{:S(2)}) collective-permute-start(f32[32,3,256]{2,1,0:T(4,128)S(1)} %get-tuple-element.110), channel_id=1, source_target_pairs={{0,1},{1,2},{2,3},{3,4},{4,5},{5,6},{6,7},{7,8},{8,9},{9,10},{10,1... | collective-permute-start | bytes 294920 | tf_op jit(solution)/shard_map/ppermute | solution.py:27
  118.2 5.9 %collective-permute-start.12 = (f32[32,3,256]{2,1,0:T(4,128)S(1)}, f32[32,3,256]{2,1,0:T(4,128)S(1)}, u32[]{:S(2)}, u32[]{:S(2)}) collective-permute-start(f32[32,3,256]{2,1,0:T(4,128)S(1)} %get-tuple-element.109), channel_id=1, source_target_pairs={{0,15},{1,0},{2,1},{3,2},{4,3},{5,4},{6,5},{7,6},{8,7},{9,8},{10,9... | collective-permute-start | bytes 294920 | tf_op jit(solution)/shard_map/ppermute | solution.py:27
  124.6 9.8 %collective-permute-start.13 = (f32[32,6,256]{2,1,0:T(8,128)S(1)}, f32[32,6,256]{2,1,0:T(8,128)S(1)}, u32[]{:S(2)}, u32[]{:S(2)}) collective-permute-start(f32[32,6,256]{2,1,0:T(8,128)S(1)} %fusion.79), channel_id=1, source_target_pairs={{128,0},{129,1},{130,2},{131,3},{132,4},{133,5},{134,6},{135,7},{1... | collective-permute-start | bytes 589832 | tf_op jit(solution)/shard_map/ppermute | solution.py:33
  145.0 5.6 %collective-permute-start.14 = (f32[32,3,256]{2,1,0:T(4,128)S(1)}, f32[32,3,256]{2,1,0:T(4,128)S(1)}, u32[]{:S(2)}, u32[]{:S(2)}) collective-permute-start(f32[32,3,256]{2,1,0:T(4,128)S(1)} %get-tuple-element.108), channel_id=1, source_target_pairs={{0,1},{1,2},{2,3},{3,4},{4,5},{5,6},{6,7},{7,8},{8,9},{9,10},{10,1... | collective-permute-start | bytes 294920 | tf_op jit(solution)/shard_map/ppermute | solution.py:27
  145.1 5.9 %collective-permute-start.15 = (f32[32,3,256]{2,1,0:T(4,128)S(1)}, f32[32,3,256]{2,1,0:T(4,128)S(1)}, u32[]{:S(2)}, u32[]{:S(2)}) collective-permute-start(f32[32,3,256]{2,1,0:T(4,128)S(1)} %get-tuple-element.107), channel_id=1, source_target_pairs={{0,15},{1,0},{2,1},{3,2},{4,3},{5,4},{6,5},{7,6},{8,7},{9,8},{10,9... | collective-permute-start | bytes 294920 | tf_op jit(solution)/shard_map/ppermute | solution.py:27
  161.9 5.6 %collective-permute-start.16 = (f32[32,3,256]{2,1,0:T(4,128)S(1)}, f32[32,3,256]{2,1,0:T(4,128)S(1)}, u32[]{:S(2)}, u32[]{:S(2)}) collective-permute-start(f32[32,3,256]{2,1,0:T(4,128)S(1)} %get-tuple-element.106), channel_id=1, source_target_pairs={{0,1},{1,2},{2,3},{3,4},{4,5},{5,6},{6,7},{7,8},{8,9},{9,10},{10,1... | collective-permute-start | bytes 294920 | tf_op jit(solution)/shard_map/ppermute | solution.py:27
  162.0 5.9 %collective-permute-start.17 = (f32[32,3,256]{2,1,0:T(4,128)S(1)}, f32[32,3,256]{2,1,0:T(4,128)S(1)}, u32[]{:S(2)}, u32[]{:S(2)}) collective-permute-start(f32[32,3,256]{2,1,0:T(4,128)S(1)} %get-tuple-element.105), channel_id=1, source_target_pairs={{0,15},{1,0},{2,1},{3,2},{4,3},{5,4},{6,5},{7,6},{8,7},{9,8},{10,9... | collective-permute-start | bytes 294920 | tf_op jit(solution)/shard_map/ppermute | solution.py:27
  168.4 4.0 %collective-permute-start.18 = (f32[32,6,128]{2,1,0:T(8,128)S(1)}, f32[32,6,128]{2,1,0:T(8,128)S(1)}, u32[]{:S(2)}, u32[]{:S(2)}) collective-permute-start(f32[32,6,128]{2,1,0:T(8,128)S(1)} %slice.329), channel_id=1, source_target_pairs={{0,128},{1,129},{2,130},{3,131},{4,132},{5,133},{6,134},{7,135},{8... | collective-permute-start | bytes 294920 | tf_op jit(solution)/shard_map/ppermute | solution.py:33
  172.4 16.3 %copy-start.1 = (f32[32,6,128]{2,0,1:T(8,128)}, f32[32,6,128]{2,0,1:T(8,128)S(1)}, u32[]{:S(2)}) copy-start(f32[32,6,128]{2,0,1:T(8,128)S(1)} %copy.38) | copy-start | bytes 294916
  173.4 14.9 %all-to-all-start = ((f32[8,32,6,128]{3,1,2,0:T(8,128)}), f32[8,32,6,128]{3,1,2,0:T(8,128)S(1)}, u32[]{:S(2)}, u32[]{:S(2)}) async-start(f32[8,32,6,128]{3,1,2,0:T(8,128)} %stack.2), calls=%async_computation | async-start | bytes 1572864 | tf_op jit(solution)/shard_map/all_to_all | solution.py:115
